TPU v7x, 32 devices: a whole 2x2x4 slice. The times are simulated.
32 devices in a mesh: rows: 8 (over z, x), rep: 4 (over y, core).
Axes of the slice: x: 2, y: 2, z: 4, core: 2. Of those that a mesh axis runs over, the one named last changes fastest.
Arguments:
- right_side: float32 [32768, 1024], P(('rep', 'rows')), parts along dimension 0, may hold values from -6 to 6
- leaf_inverse: float32 [32768, 256], P(('rep', 'rows')), parts along dimension 0, may hold values from -0.375 to 0.375
- left_factors: float32 [5, 32768, 64], P(None, ('rep', 'rows')), parts along dimension 1, may hold values from -0.75 to 0.75
- right_factors: float32 [5, 32768, 64], P(None, ('rep', 'rows')), parts along dimension 1, may hold values from -0.4375 to 0.4375, as said below
- cores: float32 [124, 128, 128], P('rep'), parts along dimension 0, may hold values from -0.5 to 0.5
Outputs:
- solution: float32 [32768, 1024], P(('rep', 'rows')), parts along dimension 0
There are 4 independent parts, one for each index of `rep`. A program takes and returns all parts, laid end to end along the dimension named above; each array names one. Nothing has to cross between parts.
Inputs may be any that keep to these rules, and one draw needn't show every extreme that they name: `right_factors`: level j's entries are of order (8192 / 2^(j+1))^(-1/2).
All inputs are finite; a program needn't handle non-finite values.
Results may differ from a plain program's by a relative error of at most 0.00016.
Values sent between devices are 32-bit elements; how exact they have to be, the bound alone decides.
A program may use at most 128 MiB of HBM per device.

v0:
```python
import jax
import jax.numpy as jnp
from jax import lax
from jax.sharding import PartitionSpec as P

HIGH = lax.Precision.HIGHEST


def swapped(value, axis, apart):
    return lax.ppermute(value, axis, [(i, i ^ 1 << apart) for i in range(lax.axis_size(axis))])


def group_level(block, left, right, cores, first, group, me):
    rank = left.shape[1]
    half_group = group // 2
    child = me // half_group % 2
    node = me // group
    core = lax.dynamic_index_in_dim(cores, first + node, 0, keepdims=False)
    own = jnp.dot(right.T, block, precision=HIGH)
    bits = group.bit_length() - 1
    mine = own
    for bit in range(bits - 1):
        width = mine.shape[1] // 2
        upper = me >> bit & 1 == 1
        keep = jnp.where(upper, mine[:, width:], mine[:, :width])
        give = jnp.where(upper, mine[:, :width], mine[:, width:])
        mine = keep + swapped(give, "rows", bit)
    other = swapped(mine, "rows", bits - 1)
    stacked = jnp.where(
        child == 0, jnp.concatenate([other, mine], 0), jnp.concatenate([mine, other], 0)
    )
    image = jnp.dot(core, stacked, precision=HIGH)
    chosen = jnp.where(child == 0, image[:rank], image[rank:])
    for bit in reversed(range(bits - 1)):
        theirs = swapped(chosen, "rows", bit)
        upper = me >> bit & 1 == 1
        chosen = jnp.where(
            upper, jnp.concatenate([theirs, chosen], 1), jnp.concatenate([chosen, theirs], 1)
        )
    return block - jnp.dot(left, chosen, precision=HIGH)


def local_level(block, left, right, cores, first, node_rows, me):
    rows_dev, cols = block.shape
    rank = left.shape[1]
    count = rows_dev // node_rows
    half = node_rows // 2
    shaped = block.reshape(count, 2, half, cols)
    basis_v = right.reshape(count, 2, half, rank)
    basis_u = left.reshape(count, 2, half, rank)
    projected = jnp.einsum("nchr,nchk->ncrk", basis_v, shaped, precision=HIGH)
    stacked = jnp.concatenate([projected[:, 1], projected[:, 0]], axis=1)
    core_set = lax.dynamic_slice_in_dim(cores, first + me * count, count, 0)
    image = jnp.einsum("nst,ntk->nsk", core_set, stacked, precision=HIGH).reshape(
        count, 2, rank, cols
    )
    update = jnp.einsum("nchr,ncrk->nchk", basis_u, image, precision=HIGH)
    return (shaped - update).reshape(rows_dev, cols)


def local(right_side, leaf_inverse, left_factors, right_factors, cores):
    n_dev = lax.axis_size("rows")
    me = lax.axis_index("rows")
    rows_dev, cols = right_side.shape
    leaf = leaf_inverse.shape[1]
    levels = left_factors.shape[0]
    blocks = rows_dev // leaf
    solved = jnp.einsum(
        "bij,bjk->bik",
        leaf_inverse.reshape(blocks, leaf, leaf),
        right_side.reshape(blocks, leaf, cols),
        precision=HIGH,
    ).reshape(rows_dev, cols)
    total = rows_dev * n_dev
    for level in reversed(range(levels)):
        node_rows = total >> level
        left = left_factors[level]
        right = right_factors[level]
        first = 2**level - 1

        def apply_level(block):
            if node_rows > rows_dev:
                return group_level(block, left, right, cores, first, node_rows // rows_dev, me)
            return local_level(block, left, right, cores, first, node_rows, me)

        solved = apply_level(solved)
    return solved


def solution(mesh):
    in_specs = (
        P(("rep", "rows"), None),
        P(("rep", "rows"), None),
        P(None, ("rep", "rows"), None),
        P(None, ("rep", "rows"), None),
        P("rep", None, None),
    )
    out_specs = P(("rep", "rows"), None)
    return jax.shard_map(local, mesh=mesh, in_specs=in_specs, out_specs=out_specs, check_vma=False)
```

profile of v0, /device:TPU:0, one launch (start us, length us, event | category | flops | bytes accessed | tf_op | source)
XLA Modules:
  0.0 128.6 jit_solution(7453532427492578503)
XLA Ops:
  0.0 1.9 %fusion.77 = (f32[1,1024,64]{1,2,0:T(8,128)}, f32[1,1024,64]{1,2,0:T(8,128)S(1)}) fusion(f32[5,1024,64]{1,2,0:T(8,128)} %param.8), kind=kLoop, calls=%fused_computation.108 | loop fusion | bytes 1048576 | tf_op jit(solution)/shard_map/slice | solution.py:78
  1.9 0.2 reshape_squeeze.8
  2.1 6.0 %fusion.78 = f32[4,256,1024]{2,1,0:T(8,128)S(1)} fusion(f32[4,256,256]{2,1,0:T(8,128)} %bitcast.96, f32[4,256,1024]{2,1,0:T(8,128)} %bitcast.95), kind=kOutput, calls=%fused_computation.109 | convolution fusion | flops 3221225472 | bytes 9437184 | tf_op jit(solution)/shard_map/bij,bjk->bik/dot_general | solution.py:68
  8.2 2.0 %copy-done.1 = f32[4,256,1024]{2,1,0:T(8,128)} copy-done((f32[4,256,1024]{2,1,0:T(8,128)}, f32[4,256,1024]{2,1,0:T(8,128)S(1)}, u32[]{:S(2)}) %copy-start.1) | copy-done | bytes 4194328
  10.2 2.8 %convolution_bitcast_fusion = f32[2,2,64,1024]{3,2,1,0:T(8,128)S(1)} fusion(f32[2,2,256,1024]{3,2,1,0:T(8,128)S(1)} %bitcast.88, f32[2,2,256,64]{2,1,0,3:T(2,128)S(1)} %reshape_squeeze.8), kind=kOutput, calls=%fused_computation.5 | convolution fusion | flops 805306368 | bytes 5505024 | tf_op jit(solution)/shard_map/nchr,nchk->ncrk/dot_general | solution.py:51
  13.0 0.1 slice_bitcast_fusion.1
  13.1 1.9 %fusion.76 = (f32[1,1024,64]{1,2,0:T(8,128)}, f32[1,1024,64]{1,2,0:T(8,128)}) fusion(f32[5,1024,64]{1,2,0:T(8,128)} %param.7), kind=kLoop, calls=%fused_computation.107 | loop fusion | bytes 1048576 | tf_op jit(solution)/shard_map/slice | solution.py:77
  15.0 1.2 reshape_squeeze.9
  16.2 1.9 %reshape.47 = f32[2,512,64]{1,0,2:T(2,128)} reshape(f32[1,1024,64]{1,2,0:T(8,128)} %get-tuple-element.7) | data formatting | bytes 524288 | tf_op jit(solution)/shard_map/reshape
  18.1 1.0 fusion
  19.1 5.5 %bitcast_subtract_fusion.4 = f32[2,2,256,1024]{3,2,1,0:T(8,128)S(1)} fusion(f32[2,2,256,1024]{3,2,1,0:T(8,128)} %bitcast.89, f32[2,2,64,1024]{3,2,1,0:T(8,128)S(1)} %bitcast.94, f32[2,2,256,64]{2,1,0,3:T(2,128)S(1)} %reshape_squeeze.9), kind=kOutput, calls=%fused_computation.4 | convolution fusion | flops 806354944 | bytes 9699328 | tf_op jit(solution)/shard_map/nchr,ncrk->nchk/dot_general | solution.py:57
  24.6 2.0 %copy-done.2 = f32[2,2,256,1024]{3,2,1,0:T(8,128)} copy-done((f32[2,2,256,1024]{3,2,1,0:T(8,128)}, f32[2,2,256,1024]{3,2,1,0:T(8,128)S(1)}, u32[]{:S(2)}) %copy-start.2) | copy-done | bytes 4194328
  26.6 2.8 %convolution_bitcast_fusion.1 = f32[1,2,64,1024]{3,2,1,0:T(8,128)S(1)} fusion(f32[2,512,1024]{2,1,0:T(8,128)S(1)} %bitcast.90, f32[2,512,64]{1,0,2:T(2,128)S(1)} %copy-done.6), kind=kOutput, calls=%fused_computation.6 | convolution fusion | flops 805306368 | bytes 4980736 | tf_op jit(solution)/shard_map/nchr,nchk->ncrk/dot_general | solution.py:51
  29.5 0.2 reshape.49
  29.7 0.6 fusion.4
  30.3 5.6 %bitcast_subtract_fusion.3 = f32[2,512,1024]{2,1,0:T(8,128)S(1)} fusion(f32[2,512,1024]{2,1,0:T(8,128)} %bitcast.91, f32[2,64,1024]{2,1,0:T(8,128)S(1)} %fusion.4, f32[2,512,64]{1,0,2:T(2,128)S(1)} %reshape.49), kind=kOutput, calls=%fused_computation.3 | convolution fusion | flops 806354944 | bytes 9175040 | tf_op jit(solution)/shard_map/nchr,ncrk->nchk/dot_general | solution.py:57
  35.9 2.0 %copy-done.5 = f32[2,512,1024]{2,1,0:T(8,128)} copy-done((f32[2,512,1024]{2,1,0:T(8,128)}, f32[2,512,1024]{2,1,0:T(8,128)S(1)}, u32[]{:S(2)}) %copy-start.5) | copy-done | bytes 4194328
  37.9 3.7 %convolution_bitcast_fusion.4 = f32[64,1024]{1,0:T(8,128)S(1)} fusion(f32[1024,1024]{1,0:T(8,128)S(1)} %bitcast.92, f32[5,1024,64]{1,2,0:T(8,128)} %param.8), kind=kOutput, calls=%fused_computation.9 | convolution fusion | flops 805306368 | bytes 4718592 | tf_op jit(solution)/shard_map/dot_general | solution.py:19
  41.6 3.0 %collective-permute-start = (f32[64,1024]{1,0:T(8,128)S(1)}, f32[64,1024]{1,0:T(8,128)S(1)}, u32[]{:S(2)}, u32[]{:S(2)}) collective-permute-start(f32[64,1024]{1,0:T(8,128)S(1)} %convolution_bitcast_fusion.4), channel_id=1, source_target_pairs={{0,4},{4,0},{8,12},{12,8},{16,20},{20,16},{24,28},{28,24},{1,5},{5... | collective-permute-start | bytes 786440 | tf_op jit(solution)/shard_map/ppermute | solution.py:10
  44.7 5.4 %copy.14 = f32[1024,1024]{0,1:T(8,128)} copy(f32[1024,1024]{1,0:T(8,128)} %bitcast.93) | data formatting | bytes 8388608 | tf_op jit(solution)/shard_map/reshape | solution.py:58
  50.0 0.9 collective-permute-done
  50.9 0.6 fusion.7
  51.5 5.4 %bitcast_subtract_fusion.2 = f32[1024,1024]{0,1:T(8,128)S(1)} fusion(f32[1024,1024]{0,1:T(8,128)} %copy.14, f32[128,1024]{1,0:T(8,128)S(1)} %fusion.7, f32[5,1024,64]{1,2,0:T(8,128)} %param.7, pred[]{:T(512)S(6)} %eq.26), kind=kOutput, calls=%fused_computation.2 | convolution fusion | flops 806420480 | bytes 9175041 | tf_op jit(solution)/shard_map/dot_general | solution.py:40
  57.0 2.0 %copy-done.4 = f32[1024,1024]{0,1:T(8,128)} copy-done((f32[1024,1024]{0,1:T(8,128)}, f32[1024,1024]{0,1:T(8,128)S(1)}, u32[]{:S(2)}) %copy-start.4) | copy-done | bytes 4194328
  59.0 5.1 %convolution_bitcast_fusion.3 = f32[64,1024]{1,0:T(8,128)S(1)} fusion(f32[1024,1024]{0,1:T(8,128)S(1)} %bitcast_subtract_fusion.2, f32[5,1024,64]{1,2,0:T(8,128)} %param.8), kind=kOutput, calls=%fused_computation.8 | convolution fusion | flops 805306368 | bytes 4718592 | tf_op jit(solution)/shard_map/dot_general | solution.py:19
  64.1 1.8 %collective-permute-start.1 = (f32[64,512]{1,0:T(8,128)S(1)}, f32[64,512]{1,0:T(8,128)S(1)}, u32[]{:S(2)}, u32[]{:S(2)}) collective-permute-start(f32[64,512]{1,0:T(8,128)S(1)} %slice_select_fusion.4), channel_id=1, source_target_pairs={{0,4},{4,0},{8,12},{12,8},{16,20},{20,16},{24,28},{28,24},{1,5},{5... | collective-permute-start | bytes 393224 | tf_op jit(solution)/shard_map/ppermute | solution.py:10
  65.9 3.2 %collective-permute-done.1 = f32[64,512]{1,0:T(8,128)S(1)} collective-permute-done((f32[64,512]{1,0:T(8,128)S(1)}, f32[64,512]{1,0:T(8,128)S(1)}, u32[]{:S(2)}, u32[]{:S(2)}) %collective-permute-start.1) | collective-permute-done | bytes 131104 | tf_op jit(solution)/shard_map/ppermute | solution.py:10
  69.2 1.9 %collective-permute-start.2 = (f32[64,512]{1,0:T(8,128)S(1)}, f32[64,512]{1,0:T(8,128)S(1)}, u32[]{:S(2)}, u32[]{:S(2)}) collective-permute-start(f32[64,512]{1,0:T(8,128)S(1)} %select_add_fusion.1), channel_id=1, source_target_pairs={{0,8},{4,12},{8,0},{12,4},{16,24},{20,28},{24,16},{28,20},{1,9},{5... | collective-permute-start | bytes 393224 | tf_op jit(solution)/shard_map/ppermute | solution.py:10
  71.1 3.1 %collective-permute-done.2 = f32[64,512]{1,0:T(8,128)S(1)} collective-permute-done((f32[64,512]{1,0:T(8,128)S(1)}, f32[64,512]{1,0:T(8,128)S(1)}, u32[]{:S(2)}, u32[]{:S(2)}) %collective-permute-start.2) | collective-permute-done | bytes 131104 | tf_op jit(solution)/shard_map/ppermute | solution.py:10
  74.2 0.4 fusion.14
  74.7 1.8 %collective-permute-start.3 = (f32[64,512]{1,0:T(8,128)S(1)}, f32[64,512]{1,0:T(8,128)S(1)}, u32[]{:S(2)}, u32[]{:S(2)}) collective-permute-start(f32[64,512]{1,0:T(8,128)S(1)} %slice_select_fusion.2), channel_id=1, source_target_pairs={{0,4},{4,0},{8,12},{12,8},{16,20},{20,16},{24,28},{28,24},{1,5},{5... | collective-permute-start | bytes 393224 | tf_op jit(solution)/shard_map/ppermute | solution.py:10
  76.5 3.2 %collective-permute-done.3 = f32[64,512]{1,0:T(8,128)S(1)} collective-permute-done((f32[64,512]{1,0:T(8,128)S(1)}, f32[64,512]{1,0:T(8,128)S(1)}, u32[]{:S(2)}, u32[]{:S(2)}) %collective-permute-start.3) | collective-permute-done | bytes 131104 | tf_op jit(solution)/shard_map/ppermute | solution.py:10
  79.7 5.4 %bitcast_subtract_fusion.1 = f32[1024,1024]{0,1:T(8,128)S(1)} fusion(f32[1024,1024]{0,1:T(8,128)} %copy-done.4, f32[64,512]{1,0:T(8,128)S(1)} %slice_select_fusion.2, f32[64,512]{1,0:T(8,128)S(1)} %collective-permute-done.3, f32[5,1024,64]{1,2,0:T(8,128)} %param.7, pred[]{:T(512)S(6)} %eq.27), kind=kOutput, calls=%fused_computation.1 | convolution fusion | flops 806551552 | bytes 8912897 | tf_op jit(solution)/shard_map/dot_general | solution.py:40
  85.1 2.0 %copy-done.3 = f32[1024,1024]{0,1:T(8,128)} copy-done((f32[1024,1024]{0,1:T(8,128)}, f32[1024,1024]{0,1:T(8,128)S(1)}, u32[]{:S(2)}) %copy-start.3) | copy-done | bytes 4194328
  87.1 5.1 %convolution_bitcast_fusion.2 = f32[64,1024]{1,0:T(8,128)S(1)} fusion(f32[1024,1024]{0,1:T(8,128)S(1)} %bitcast_subtract_fusion.1, f32[5,1024,64]{1,2,0:T(8,128)} %param.8), kind=kOutput, calls=%fused_computation.7 | convolution fusion | flops 805306368 | bytes 4718592 | tf_op jit(solution)/shard_map/dot_general | solution.py:19
  92.3 1.8 %collective-permute-start.4 = (f32[64,512]{1,0:T(8,128)S(1)}, f32[64,512]{1,0:T(8,128)S(1)}, u32[]{:S(2)}, u32[]{:S(2)}) collective-permute-start(f32[64,512]{1,0:T(8,128)S(1)} %slice_select_fusion.3), channel_id=1, source_target_pairs={{0,4},{4,0},{8,12},{12,8},{16,20},{20,16},{24,28},{28,24},{1,5},{5... | collective-permute-start | bytes 393224 | tf_op jit(solution)/shard_map/ppermute | solution.py:10
  94.1 3.2 %collective-permute-done.4 = f32[64,512]{1,0:T(8,128)S(1)} collective-permute-done((f32[64,512]{1,0:T(8,128)S(1)}, f32[64,512]{1,0:T(8,128)S(1)}, u32[]{:S(2)}, u32[]{:S(2)}) %collective-permute-start.4) | collective-permute-done | bytes 131104 | tf_op jit(solution)/shard_map/ppermute | solution.py:10
  97.4 1.9 %collective-permute-start.5 = (f32[64,256]{1,0:T(8,128)S(1)}, f32[64,256]{1,0:T(8,128)S(1)}, u32[]{:S(2)}, u32[]{:S(2)}) collective-permute-start(f32[64,256]{1,0:T(8,128)S(1)} %slice_select_fusion.6), channel_id=1, source_target_pairs={{0,8},{4,12},{8,0},{12,4},{16,24},{20,28},{24,16},{28,20},{1,9},{5... | collective-permute-start | bytes 196616 | tf_op jit(solution)/shard_map/ppermute | solution.py:10
  99.3 2.4 %collective-permute-done.5 = f32[64,256]{1,0:T(8,128)S(1)} collective-permute-done((f32[64,256]{1,0:T(8,128)S(1)}, f32[64,256]{1,0:T(8,128)S(1)}, u32[]{:S(2)}, u32[]{:S(2)}) %collective-permute-start.5) | collective-permute-done | bytes 65568 | tf_op jit(solution)/shard_map/ppermute | solution.py:10
  101.7 2.9 %collective-permute-start.6 = (f32[64,256]{1,0:T(8,128)S(1)}, f32[64,256]{1,0:T(8,128)S(1)}, u32[]{:S(2)}, u32[]{:S(2)}) collective-permute-start(f32[64,256]{1,0:T(8,128)S(1)} %select_add_fusion.2), channel_id=1, source_target_pairs={{0,16},{4,20},{8,24},{12,28},{16,0},{20,4},{24,8},{28,12},{1,17},{... | collective-permute-start | bytes 196616 | tf_op jit(solution)/shard_map/ppermute | solution.py:10
  104.6 2.3 %collective-permute-done.6 = f32[64,256]{1,0:T(8,128)S(1)} collective-permute-done((f32[64,256]{1,0:T(8,128)S(1)}, f32[64,256]{1,0:T(8,128)S(1)}, u32[]{:S(2)}, u32[]{:S(2)}) %collective-permute-start.6) | collective-permute-done | bytes 65568 | tf_op jit(solution)/shard_map/ppermute | solution.py:10
  106.9 0.3 fusion.47
  107.2 1.9 %collective-permute-start.7 = (f32[64,256]{1,0:T(8,128)S(1)}, f32[64,256]{1,0:T(8,128)S(1)}, u32[]{:S(2)}, u32[]{:S(2)}) collective-permute-start(f32[64,256]{1,0:T(8,128)S(1)} %slice_select_fusion.5), channel_id=1, source_target_pairs={{0,8},{4,12},{8,0},{12,4},{16,24},{20,28},{24,16},{28,20},{1,9},{5... | collective-permute-start | bytes 196616 | tf_op jit(solution)/shard_map/ppermute | solution.py:10
  109.1 2.4 %collective-permute-done.7 = f32[64,256]{1,0:T(8,128)S(1)} collective-permute-done((f32[64,256]{1,0:T(8,128)S(1)}, f32[64,256]{1,0:T(8,128)S(1)}, u32[]{:S(2)}, u32[]{:S(2)}) %collective-permute-start.7) | collective-permute-done | bytes 65568 | tf_op jit(solution)/shard_map/ppermute | solution.py:10
  111.6 1.8 %collective-permute-start.8 = (f32[64,512]{1,0:T(8,128)S(1)}, f32[64,512]{1,0:T(8,128)S(1)}, u32[]{:S(2)}, u32[]{:S(2)}) collective-permute-start(f32[64,512]{1,0:T(8,128)S(1)} %maximum_select_fusion.10), channel_id=1, source_target_pairs={{0,4},{4,0},{8,12},{12,8},{16,20},{20,16},{24,28},{28,24},{1,5},{5... | collective-permute-start | bytes 393224 | tf_op jit(solution)/shard_map/ppermute | solution.py:10
  113.4 3.2 %collective-permute-done.8 = f32[64,512]{1,0:T(8,128)S(1)} collective-permute-done((f32[64,512]{1,0:T(8,128)S(1)}, f32[64,512]{1,0:T(8,128)S(1)}, u32[]{:S(2)}, u32[]{:S(2)}) %collective-permute-start.8) | collective-permute-done | bytes 131104 | tf_op jit(solution)/shard_map/ppermute | solution.py:10
  116.6 6.6 %bitcast_subtract_fusion = f32[1024,1024]{0,1:T(8,128)} fusion(f32[1024,1024]{0,1:T(8,128)} %copy-done.3, f32[64,512]{1,0:T(8,128)S(1)} %maximum_select_fusion.10, f32[64,512]{1,0:T(8,128)S(1)} %collective-permute-done.8, f32[5,1024,64]{1,2,0:T(8,128)} %param.7, pred[]{:T(512)S(6)} %eq.27), kind=kOutput, calls=%fused_computation | convolution fusion | flops 806551552 | bytes 8912897 | tf_op jit(solution)/shard_map/dot_general | solution.py:40
  123.2 5.3 %copy.15 = f32[1024,1024]{1,0:T(8,128)} copy(f32[1024,1024]{0,1:T(8,128)} %bitcast_subtract_fusion) | data formatting | bytes 8388608 | tf_op jit(solution)/shard_map/sub | solution.py:40
  (22 shorter events, 0.2 us)
Async XLA Ops:
  0.0 18.0 %copy-start = (f32[31,128,128]{2,1,0:T(8,128)S(1)}, f32[31,128,128]{2,1,0:T(8,128)}, u32[]{:S(2)}) copy-start(f32[31,128,128]{2,1,0:T(8,128)} %param.9) | copy-start | bytes 6094852
  8.2 2.0 %copy-start.1 = (f32[4,256,1024]{2,1,0:T(8,128)}, f32[4,256,1024]{2,1,0:T(8,128)S(1)}, u32[]{:S(2)}) copy-start(f32[4,256,1024]{2,1,0:T(8,128)S(1)} %fusion.78) | copy-start | bytes 12582916
  19.1 7.5 %copy-start.6 = (f32[2,512,64]{1,0,2:T(2,128)S(1)}, f32[2,512,64]{1,0,2:T(2,128)}, u32[]{:S(2)}) copy-start(f32[2,512,64]{1,0,2:T(2,128)} %reshape.47) | copy-start | bytes 786436
  24.6 2.0 %copy-start.2 = (f32[2,2,256,1024]{3,2,1,0:T(8,128)}, f32[2,2,256,1024]{3,2,1,0:T(8,128)S(1)}, u32[]{:S(2)}) copy-start(f32[2,2,256,1024]{3,2,1,0:T(8,128)S(1)} %bitcast_subtract_fusion.4) | copy-start | bytes 12582916
  24.6 4.9 %copy-start.7 = (f32[1,1024,64]{1,2,0:T(8,128)S(1)}, f32[1,1024,64]{1,2,0:T(8,128)}, u32[]{:S(2)}) copy-start(f32[1,1024,64]{1,2,0:T(8,128)} %get-tuple-element.5) | copy-start | bytes 786436
  35.9 2.0 %copy-start.5 = (f32[2,512,1024]{2,1,0:T(8,128)}, f32[2,512,1024]{2,1,0:T(8,128)S(1)}, u32[]{:S(2)}) copy-start(f32[2,512,1024]{2,1,0:T(8,128)S(1)} %bitcast_subtract_fusion.3) | copy-start | bytes 12582916
  41.6 9.3 %collective-permute-start = (f32[64,1024]{1,0:T(8,128)S(1)}, f32[64,1024]{1,0:T(8,128)S(1)}, u32[]{:S(2)}, u32[]{:S(2)}) collective-permute-start(f32[64,1024]{1,0:T(8,128)S(1)} %convolution_bitcast_fusion.4), channel_id=1, source_target_pairs={{0,4},{4,0},{8,12},{12,8},{16,20},{20,16},{24,28},{28,24},{1,5},{5... | collective-permute-start | bytes 786440 | tf_op jit(solution)/shard_map/ppermute | solution.py:10
  57.0 2.0 %copy-start.4 = (f32[1024,1024]{0,1:T(8,128)}, f32[1024,1024]{0,1:T(8,128)S(1)}, u32[]{:S(2)}) copy-start(f32[1024,1024]{0,1:T(8,128)S(1)} %bitcast_subtract_fusion.2) | copy-start | bytes 12582916
  64.1 5.0 %collective-permute-start.1 = (f32[64,512]{1,0:T(8,128)S(1)}, f32[64,512]{1,0:T(8,128)S(1)}, u32[]{:S(2)}, u32[]{:S(2)}) collective-permute-start(f32[64,512]{1,0:T(8,128)S(1)} %slice_select_fusion.4), channel_id=1, source_target_pairs={{0,4},{4,0},{8,12},{12,8},{16,20},{20,16},{24,28},{28,24},{1,5},{5... | collective-permute-start | bytes 393224 | tf_op jit(solution)/shard_map/ppermute | solution.py:10
  69.2 5.0 %collective-permute-start.2 = (f32[64,512]{1,0:T(8,128)S(1)}, f32[64,512]{1,0:T(8,128)S(1)}, u32[]{:S(2)}, u32[]{:S(2)}) collective-permute-start(f32[64,512]{1,0:T(8,128)S(1)} %select_add_fusion.1), channel_id=1, source_target_pairs={{0,8},{4,12},{8,0},{12,4},{16,24},{20,28},{24,16},{28,20},{1,9},{5... | collective-permute-start | bytes 393224 | tf_op jit(solution)/shard_map/ppermute | solution.py:10
  74.7 5.0 %collective-permute-start.3 = (f32[64,512]{1,0:T(8,128)S(1)}, f32[64,512]{1,0:T(8,128)S(1)}, u32[]{:S(2)}, u32[]{:S(2)}) collective-permute-start(f32[64,512]{1,0:T(8,128)S(1)} %slice_select_fusion.2), channel_id=1, source_target_pairs={{0,4},{4,0},{8,12},{12,8},{16,20},{20,16},{24,28},{28,24},{1,5},{5... | collective-permute-start | bytes 393224 | tf_op jit(solution)/shard_map/ppermute | solution.py:10
  85.1 2.0 %copy-start.3 = (f32[1024,1024]{0,1:T(8,128)}, f32[1024,1024]{0,1:T(8,128)S(1)}, u32[]{:S(2)}) copy-start(f32[1024,1024]{0,1:T(8,128)S(1)} %bitcast_subtract_fusion.1) | copy-start | bytes 12582916
  92.3 5.0 %collective-permute-start.4 = (f32[64,512]{1,0:T(8,128)S(1)}, f32[64,512]{1,0:T(8,128)S(1)}, u32[]{:S(2)}, u32[]{:S(2)}) collective-permute-start(f32[64,512]{1,0:T(8,128)S(1)} %slice_select_fusion.3), channel_id=1, source_target_pairs={{0,4},{4,0},{8,12},{12,8},{16,20},{20,16},{24,28},{28,24},{1,5},{5... | collective-permute-start | bytes 393224 | tf_op jit(solution)/shard_map/ppermute | solution.py:10
  97.4 4.3 %collective-permute-start.5 = (f32[64,256]{1,0:T(8,128)S(1)}, f32[64,256]{1,0:T(8,128)S(1)}, u32[]{:S(2)}, u32[]{:S(2)}) collective-permute-start(f32[64,256]{1,0:T(8,128)S(1)} %slice_select_fusion.6), channel_id=1, source_target_pairs={{0,8},{4,12},{8,0},{12,4},{16,24},{20,28},{24,16},{28,20},{1,9},{5... | collective-permute-start | bytes 196616 | tf_op jit(solution)/shard_map/ppermute | solution.py:10
  101.7 5.2 %collective-permute-start.6 = (f32[64,256]{1,0:T(8,128)S(1)}, f32[64,256]{1,0:T(8,128)S(1)}, u32[]{:S(2)}, u32[]{:S(2)}) collective-permute-start(f32[64,256]{1,0:T(8,128)S(1)} %select_add_fusion.2), channel_id=1, source_target_pairs={{0,16},{4,20},{8,24},{12,28},{16,0},{20,4},{24,8},{28,12},{1,17},{... | collective-permute-start | bytes 196616 | tf_op jit(solution)/shard_map/ppermute | solution.py:10
  107.2 4.3 %collective-permute-start.7 = (f32[64,256]{1,0:T(8,128)S(1)}, f32[64,256]{1,0:T(8,128)S(1)}, u32[]{:S(2)}, u32[]{:S(2)}) collective-permute-start(f32[64,256]{1,0:T(8,128)S(1)} %slice_select_fusion.5), channel_id=1, source_target_pairs={{0,8},{4,12},{8,0},{12,4},{16,24},{20,28},{24,16},{28,20},{1,9},{5... | collective-permute-start | bytes 196616 | tf_op jit(solution)/shard_map/ppermute | solution.py:10
  111.6 5.0 %collective-permute-start.8 = (f32[64,512]{1,0:T(8,128)S(1)}, f32[64,512]{1,0:T(8,128)S(1)}, u32[]{:S(2)}, u32[]{:S(2)}) collective-permute-start(f32[64,512]{1,0:T(8,128)S(1)} %maximum_select_fusion.10), channel_id=1, source_target_pairs={{0,4},{4,0},{8,12},{12,8},{16,20},{20,16},{24,28},{28,24},{1,5},{5... | collective-permute-start | bytes 393224 | tf_op jit(solution)/shard_map/ppermute | solution.py:10
where the time goes:
time: 129 us
  matrix products  57 us (44%)
  local copies, waits for them, and re-layouts  28.2 us (22%)
  waiting for transfers between devices  24.2 us (19%)
  starting transfers between devices  18.8 us (15%)
    ppermute x9, waiting for transfers between devices, swapped(): lax.ppermute(value, axis, [(i, i ^ 1 << apart) for i in range(lax.axis_si...  24.2 us
    ppermute x9, starting transfers between devices, swapped(): lax.ppermute(value, axis, [(i, i ^ 1 << apart) for i in range(lax.axis_si...  18.8 us
    dot_general x3, matrix products, group_level(): return block - jnp.dot(left, chosen, precision=HIGH)  17.5 us
    dot_general x3, matrix products, group_level(): own = jnp.dot(right.T, block, precision=HIGH)  14 us
    dot_general x2, matrix products, local_level(): update = jnp.einsum('nchr,ncrk->nchk', basis_u, image, precision=HIGH)  11.1 us
    unnamed x16, local copies, waits for them, and re-layouts  10 us
    dot_general x1, matrix products, local(): jnp.einsum('bij,bjk->bik', leaf_inverse.reshape(blocks, leaf, leaf), righ...  6 us
    dot_general x2, matrix products, local_level(): projected = jnp.einsum('nchr,nchk->ncrk', basis_v, shaped, precision=HIGH)  5.66 us
  transfers between devices with their start and end apart: 9, of which 9 were waited for; matrix products, arithmetic and copies ran while one was open for 4% of the time, Pallas kernels for 0%

commit v1 on v0

v1 whole, which is shorter than its diff:
```python
import functools

import jax
import jax.numpy as jnp
from jax import lax
from jax.experimental import pallas as pl
from jax.experimental.pallas import tpu as pltpu
from jax.sharding import PartitionSpec as P

LANES = 128
CHUNK = 2 * LANES
HIGH = lax.Precision.HIGH
F32 = jnp.float32


def dot(a, b):
    return jnp.dot(a, b, precision=HIGH, preferred_element_type=F32)


def dot_nt(a, b):
    return lax.dot_general(
        a, b, (((1,), (1,)), ((), ())), precision=HIGH, preferred_element_type=F32
    )


def split(x):
    high = x.astype(jnp.bfloat16)
    return high, (x - high.astype(F32)).astype(jnp.bfloat16)


def level_order(bits, levels):
    return [bits - 1 - s for s in range(bits)] + list(range(bits, levels))


def local_offset(level, bits, rank):
    return rank * (2 ** (level - bits + 1) - 2)


def tree_kernel(bits, levels, blocks, right_hbm, leaf_hbm, vt_ref, ut_ref, cores_hbm, *refs):
    local_levels = list(range(bits, levels))
    refs = list(refs)
    qg_ref = refs.pop(0)
    ql_ref = refs.pop(0) if local_levels else None
    rbuf, leaf, core_g, m_ref, sem_in = refs[:5]
    gram_out, gram_in, first_out, first_in, later_out, later_in, q_out, q_in, qfull = refs[5:14]
    gram_sem, first_sem, later_sem, q_sem = refs[14:18]
    core_l = refs[18 : 18 + len(local_levels)]
    ch_refs = refs[18 + len(local_levels) :]

    me = lax.axis_index("rows")
    rows_dev = vt_ref.shape[2]
    rank = vt_ref.shape[1]
    chunks = rbuf.shape[0]
    lf = rows_dev // blocks
    upper = lax.rem(me, 2) == 1
    order = level_order(bits, levels)

    def child(s):
        return lax.rem(me // 2**s, 2)

    def partner(s):
        return me + (1 - 2 * child(s)) * 2**s

    loads = []
    slot = 0

    def load(src, dst):
        nonlocal slot
        copy = pltpu.make_async_copy(src, dst, sem_in.at[slot])
        slot += 1
        copy.start()
        return copy

    loads.append(load(leaf_hbm, leaf))
    for s in range(bits):
        level = bits - 1 - s
        loads.append(load(cores_hbm.at[2**level - 1 + me // 2 ** (s + 1)], core_g.at[s]))
    for n, level in enumerate(local_levels):
        count = 2 ** (level - bits)
        loads.append(load(cores_hbm.at[pl.ds(2**level - 1 + me * count, count)], core_l[n]))
    right_loads = [
        load(right_hbm.at[:, pl.ds(c * CHUNK, CHUNK)], rbuf.at[c]) for c in range(chunks)
    ]

    barrier = pltpu.get_barrier_semaphore()
    for s in range(bits):
        pl.semaphore_signal(
            barrier, inc=1, device_id={"rows": partner(s)}, device_id_type=pl.DeviceIdType.MESH
        )
    pl.semaphore_wait(barrier, bits)

    sent = []

    def send(src, dst, sems, s):
        copy = pltpu.make_async_remote_copy(
            src_ref=src,
            dst_ref=dst,
            send_sem=sems.at[0],
            recv_sem=sems.at[1],
            device_id={"rows": partner(s)},
            device_id_type=pl.DeviceIdType.MESH,
        )
        copy.start()
        sent.append(copy)
        return copy

    gram_cols = gram_out.shape[2]
    u_rows = [ut_ref[bits - 1 - s] for s in range(bits - 1)]
    pad = gram_cols - rank * (bits - 1)
    if pad:
        u_rows.append(jnp.zeros((pad, rows_dev), F32))
    v_rows = [vt_ref[bits - 1 - s] for s in range(1, bits)]
    gram_out[0] = dot_nt(jnp.concatenate(v_rows, 0), jnp.concatenate(u_rows, 0))
    gram_copy = {0: send(gram_out.at[0], gram_in.at[0], gram_sem.at[0], 0)}

    for copy in loads:
        copy.wait()
    vt_all = jnp.concatenate([vt_ref[level] for level in order], 0)
    for i in range(blocks):
        cols = slice(i * lf, (i + 1) * lf)
        m_ref[i] = dot(vt_all[:, cols], leaf[cols, :])
    for n, level in enumerate(local_levels):
        count = 2 ** (level - bits)
        node = rows_dev // count
        half = node // 2
        zero = jnp.zeros((rank, half), F32)
        for k in range(count):
            base = k * node
            u_a = ut_ref[level, :, base : base + half]
            u_b = ut_ref[level, :, base + half : base + node]
            diag = jnp.concatenate(
                [jnp.concatenate([u_a, zero], 1), jnp.concatenate([zero, u_b], 1)], 0
            )
            gram = dot_nt(vt_all[: rank * level, base : base + node], diag)
            core = core_l[n][k]
            ch_refs[n][k, : 2 * rank] = core
            ch_refs[n][k, 2 * rank :] = dot(gram, core)

    first_copy, later_copy, q_copy = {}, {}, {}

    def forward(c):
        right_loads[c].wait()
        parts = [dot(m_ref[i], rbuf[c, i * lf : (i + 1) * lf, :]) for i in range(blocks)]
        for n in reversed(range(len(local_levels))):
            level = local_levels[n]
            top = rank * level
            merged = []
            for k in range(len(parts) // 2):
                a, b = parts[2 * k], parts[2 * k + 1]
                image = dot(ch_refs[n][k], jnp.concatenate([b[top:], a[top:]], 0))
                start = local_offset(level, bits, rank) + 2 * rank * k
                ql_ref[start : start + 2 * rank, c * CHUNK : (c + 1) * CHUNK] = image[: 2 * rank]
                merged.append(a[:top] + b[:top] - image[2 * rank :])
            parts = merged
        p = parts[0]
        low, high = p[:, :LANES], p[:, LANES:]
        first_out[c, :rank] = low[:rank]
        first_out[c, rank : 2 * rank] = high[:rank]
        first_out[c, 2 * rank :] = jnp.where(upper, low[rank:], high[rank:])
        first_copy[c] = send(first_out.at[c], first_in.at[c], first_sem.at[c], 0)
        later_out[0, c] = jnp.where(upper, high[rank:], low[rank:])

    def stack(mine, theirs, s):
        first = child(s) == 0
        return jnp.concatenate([jnp.where(first, theirs, mine), jnp.where(first, mine, theirs)], 0)

    def pick(image, s):
        first = child(s) == 0
        return (
            jnp.where(first, image[:rank], image[rank:]),
            jnp.where(first, image[rank:], image[:rank]),
        )

    def correction(s, own, sib):
        zeros = [jnp.zeros((rank, LANES), F32)]
        before, after = s, gram_cols // rank - 1 - s
        rows = slice(rank * s, None)
        q_own = jnp.concatenate(zeros * before + [own] + zeros * after, 0)
        q_sib = jnp.concatenate(zeros * before + [sib] + zeros * after, 0)
        return dot(gram_out[s, rows, :], q_own) + dot(gram_in[s, rows, :], q_sib)

    def grams(s):
        gram_copy[s].wait_recv()
        if s + 1 < bits - 1:
            gram_out[s + 1] = gram_out[s] + gram_in[s]
            gram_copy[s + 1] = send(
                gram_out.at[s + 1], gram_in.at[s + 1], gram_sem.at[s + 1], s + 1
            )

    def step(s, c):
        if c == 0 and s < bits - 1:
            grams(s)
        if s == 0:
            first_copy[c].wait_recv()
            mine = jnp.concatenate([first_out[c, :rank], first_out[c, rank : 2 * rank]], 1)
            theirs = jnp.concatenate([first_in[c, :rank], first_in[c, rank : 2 * rank]], 1)
            image = dot(core_g[0], stack(mine, theirs, 0))
            own, sib = pick(image, 0)
            qfull[0, :, c * CHUNK : (c + 1) * CHUNK] = own
            own = jnp.where(upper, own[:, LANES:], own[:, :LANES])
            sib = jnp.where(upper, sib[:, LANES:], sib[:, :LANES])
            rest = later_out[0, c] + first_in[c, 2 * rank :]
        else:
            later_copy[s, c].wait_recv()
            live = slice(rank * (s - 1), rank * s)
            image = dot(core_g[s], stack(later_out[s, c, live], later_in[s, c, live], s))
            own, sib = pick(image, s)
            q_out[s - 1, c] = own
            q_copy[s, c] = send(q_out.at[s - 1, c], q_in.at[s - 1, c], q_sem.at[s - 1, c], 0)
            if s < bits - 1:
                rest = later_out[s, c, rank * s :] + later_in[s, c, rank * s :]
        if s < bits - 1:
            later_out[s + 1, c, rank * s :] = rest - correction(s, own, sib)
            later_copy[s + 1, c] = send(
                later_out.at[s + 1, c, pl.ds(rank * s, rank * (bits - 1 - s))],
                later_in.at[s + 1, c, pl.ds(rank * s, rank * (bits - 1 - s))],
                later_sem.at[s, c],
                s + 1,
            )

    def finish(s, c):
        q_copy[s, c].wait_recv()
        own, other = q_out[s - 1, c], q_in[s - 1, c]
        qfull[s, :, c * CHUNK : c * CHUNK + LANES] = jnp.where(upper, other, own)
        qfull[s, :, c * CHUNK + LANES : (c + 1) * CHUNK] = jnp.where(upper, own, other)

    for t in range(chunks + bits):
        if t < chunks:
            forward(t)
        for s in range(bits):
            c = t - 1 - s
            if 0 <= c < chunks:
                step(s, c)
    for c in range(chunks):
        for s in range(1, bits):
            finish(s, c)
    for s in range(bits):
        qg_ref[s * rank : (s + 1) * rank] = qfull[s]
    for copy in sent:
        copy.wait_send()


def tree(bits, right_side, leaf_inverse, vt, ut, cores):
    rows_dev, cols = right_side.shape
    lf = leaf_inverse.shape[1]
    levels, rank = vt.shape[:2]
    blocks = rows_dev // lf
    chunks = cols // CHUNK
    local_levels = list(range(bits, levels))
    assert blocks == 2 ** len(local_levels) and bits >= 2
    gram_cols = pl.cdiv(rank * (bits - 1), LANES) * LANES
    out_shape = [jax.ShapeDtypeStruct((rank * bits, cols), F32)]
    if local_levels:
        out_shape.append(jax.ShapeDtypeStruct((rank * (2 * blocks - 2), cols), F32))
    vmem = pl.BlockSpec(memory_space=pltpu.VMEM)
    hbm = pl.BlockSpec(memory_space=pl.ANY)
    counts = [2 ** (level - bits) for level in local_levels]
    rest = rank * (bits - 1)
    scratch = [
        pltpu.VMEM((chunks, rows_dev, CHUNK), F32),
        pltpu.VMEM((rows_dev, lf), F32),
        pltpu.VMEM((bits, 2 * rank, 2 * rank), F32),
        pltpu.VMEM((blocks, levels * rank, lf), F32),
        pltpu.SemaphoreType.DMA((1 + levels + chunks,)),
        pltpu.VMEM((bits - 1, rest, gram_cols), F32),
        pltpu.VMEM((bits - 1, rest, gram_cols), F32),
        pltpu.VMEM((chunks, 2 * rank + rest, LANES), F32),
        pltpu.VMEM((chunks, 2 * rank + rest, LANES), F32),
        pltpu.VMEM((bits, chunks, rest, LANES), F32),
        pltpu.VMEM((bits, chunks, rest, LANES), F32),
        pltpu.VMEM((bits - 1, chunks, rank, LANES), F32),
        pltpu.VMEM((bits - 1, chunks, rank, LANES), F32),
        pltpu.VMEM((bits, rank, cols), F32),
        pltpu.SemaphoreType.DMA((bits - 1, 2)),
        pltpu.SemaphoreType.DMA((chunks, 2)),
        pltpu.SemaphoreType.DMA((bits - 1, chunks, 2)),
        pltpu.SemaphoreType.DMA((bits - 1, chunks, 2)),
    ]
    scratch += [pltpu.VMEM((count, 2 * rank, 2 * rank), F32) for count in counts]
    scratch += [
        pltpu.VMEM((count, rank * (level + 2), 2 * rank), F32)
        for count, level in zip(counts, local_levels)
    ]
    return pl.pallas_call(
        functools.partial(tree_kernel, bits, levels, blocks),
        out_shape=out_shape,
        in_specs=[hbm, hbm, vmem, vmem, hbm],
        out_specs=[vmem] * len(out_shape),
        scratch_shapes=scratch,
        compiler_params=pltpu.CompilerParams(
            collective_id=0, has_side_effects=True, vmem_limit_bytes=56 << 20
        ),
        name="tree",
    )(right_side, leaf_inverse, vt, ut, cores)


def apply_kernel(bits, levels, blocks, right_ref, leaf_ref, ut_ref, qg_ref, *refs):
    ql_ref = refs[0] if levels > bits else None
    out_ref, high_ref, low_ref = refs[-3:]
    rank, rows_dev = ut_ref.shape[1:]
    lf = rows_dev // blocks
    pad = high_ref.shape[1] - lf - levels * rank

    @pl.when(pl.program_id(0) == 0)
    def _():
        high, low = split(leaf_ref[...])
        high_ref[:, :lf] = high
        low_ref[:, :lf] = low
        rows = [ut_ref[level] for level in level_order(bits, levels)]
        if pad:
            rows.append(jnp.zeros((pad, rows_dev), F32))
        high, low = split(-jnp.concatenate(rows, 0).T)
        high_ref[:, lf:] = high
        low_ref[:, lf:] = low

    q_high, q_low = split(qg_ref[...])
    if ql_ref is not None:
        l_high, l_low = split(ql_ref[...])
    zero = [jnp.zeros((pad, out_ref.shape[1]), jnp.bfloat16)] if pad else []
    for i in range(blocks):
        rows = slice(i * lf, (i + 1) * lf)
        x_high, x_low = split(right_ref[rows, :])
        highs, lows = [x_high, q_high], [x_low, q_low]
        for level in range(bits, levels):
            start = local_offset(level, bits, rank) + rank * (i * 2 ** (level - bits + 1) // blocks)
            highs.append(l_high[start : start + rank])
            lows.append(l_low[start : start + rank])
        x_high = jnp.concatenate(highs + zero, 0)
        x_low = jnp.concatenate(lows + zero, 0)
        a_high, a_low = high_ref[rows, :], low_ref[rows, :]
        out_ref[rows, :] = (
            jnp.dot(a_high, x_high, preferred_element_type=F32)
            + jnp.dot(a_high, x_low, preferred_element_type=F32)
            + jnp.dot(a_low, x_high, preferred_element_type=F32)
        )


def apply(bits, right_side, leaf_inverse, ut, qs):
    rows_dev, cols = right_side.shape
    lf = leaf_inverse.shape[1]
    levels, rank = ut.shape[:2]
    blocks = rows_dev // lf
    depth = lf + pl.cdiv(levels * rank, LANES) * LANES
    width = CHUNK

    def column(rows):
        return pl.BlockSpec((rows, width), lambda c: (0, c))

    return pl.pallas_call(
        functools.partial(apply_kernel, bits, levels, blocks),
        grid=(cols // width,),
        out_shape=jax.ShapeDtypeStruct((rows_dev, cols), F32),
        in_specs=[
            column(rows_dev),
            pl.BlockSpec((rows_dev, lf), lambda c: (0, 0)),
            pl.BlockSpec(ut.shape, lambda c: (0, 0, 0)),
        ]
        + [column(q.shape[0]) for q in qs],
        out_specs=column(rows_dev),
        scratch_shapes=[pltpu.VMEM((rows_dev, depth), jnp.bfloat16)] * 2,
        compiler_params=pltpu.CompilerParams(vmem_limit_bytes=56 << 20),
        name="apply",
    )(right_side, leaf_inverse, ut, *qs)


def local(bits, right_side, leaf_inverse, left_factors, right_factors, cores):
    ut = jnp.swapaxes(left_factors, 1, 2)
    vt = jnp.swapaxes(right_factors, 1, 2)
    qs = tree(bits, right_side, leaf_inverse, vt, ut, cores)
    return apply(bits, right_side, leaf_inverse, ut, qs)


def solution(mesh):
    bits = mesh.shape["rows"].bit_length() - 1
    in_specs = (
        P(("rep", "rows"), None),
        P(("rep", "rows"), None),
        P(None, ("rep", "rows"), None),
        P(None, ("rep", "rows"), None),
        P("rep", None, None),
    )
    out_specs = P(("rep", "rows"), None)
    return jax.shard_map(
        functools.partial(local, bits),
        mesh=mesh,
        in_specs=in_specs,
        out_specs=out_specs,
        check_vma=False,
    )
```

time: 129 us -> 49.2 us (0.38)
  matrix products: 57 us -> 0 us
  Pallas kernels: 0 us -> 48.9 us
  local copies, waits for them, and re-layouts: 28.2 us -> 0 us
  waiting for transfers between devices: 24.2 us -> 0 us
  starting transfers between devices: 18.8 us -> 0 us
    dot_general x16 -> x0, matrix products: 57 us -> none  [the longest x3 17.5 us: group_level(): return block - jnp.dot(left, chosen, precision=HIGH)]
    pallas_call x0 -> x2, Pallas kernels: none -> 48.9 us  [the longest x1 38.9 us: tree(): pl.pallas_call(functools.partial(tree_kernel, bits, levels, blocks), out_...]
    ppermute x9 -> x0, waiting for transfers between devices: 24.2 us -> none  [swapped(): lax.ppermute(value, axis, [(i, i ^ 1 << apart) for i in range(lax.axis_si...]
    ppermute x9 -> x0, starting transfers between devices: 18.8 us -> none  [swapped(): lax.ppermute(value, axis, [(i, i ^ 1 << apart) for i in range(lax.axis_si...]
    unnamed x16 -> x0, local copies, waits for them, and re-layouts: 10 us -> none
    reshape x2 -> x0, local copies, waits for them, and re-layouts: 7.23 us -> none  [the longest x1 5.36 us: local_level(): return (shaped - update).reshape(rows_dev, cols)]
    sub x1 -> x0, local copies, waits for them, and re-layouts: 5.34 us -> none  [group_level(): return block - jnp.dot(left, chosen, precision=HIGH)]
    slice x2 -> x0, local copies, waits for them, and re-layouts: 3.8 us -> none  [the longest x1 1.92 us: local(): right = right_factors[level]]
  transfers between devices with their start and end apart: 9 -> 0, of which waited for: 9 -> 0; matrix products, arithmetic and copies ran while one was open for 4% -> 0% of each run, Pallas kernels for 0% -> 0%
where the time goes in v1:
time: 49.2 us; the launch traced here: 48.9 us
  Pallas kernels  48.9 us (99%)
    pallas_call x1, Pallas kernels, tree(): pl.pallas_call(functools.partial(tree_kernel, bits, levels, blocks), out_...  38.9 us
    pallas_call x1, Pallas kernels, apply(): pl.pallas_call(functools.partial(apply_kernel, bits, levels, blocks), gri...  10.1 us

profile of v1, /device:TPU:0, one launch (start us, length us, event | category | flops | bytes accessed | tf_op | source)
XLA Modules:
  0.0 48.9 jit_solution(16131410244104911364)
XLA Ops:
  0.0 38.9 %tree.1 = (f32[192,1024]{1,0:T(8,128)}, f32[384,1024]{1,0:T(8,128)}) custom-call(f32[1024,1024]{1,0:T(8,128)} %right_ref.1, f32[1024,256]{1,0:T(8,128)} %leaf_ref.1, f32[5,64,1024]{2,1,0:T(8,128)} %bitcast.4, f32[5,64,1024]{2,1,0:T(8,128)} %bitcast.2, f32[31,128,128]{2,1,0:T(8,128)} %cores_hbm.1), custom_call_target="tpu_custom_call" | custom-call | tf_op jit(solution)/shard_map/tree/pallas_call | solution.py:284
  38.9 10.1 %apply.1 = f32[1024,1024]{1,0:T(8,128)} custom-call(f32[1024,1024]{1,0:T(8,128)} %right_ref.1, f32[1024,256]{1,0:T(8,128)} %leaf_ref.1, f32[5,64,1024]{2,1,0:T(8,128)} %bitcast.3, f32[192,1024]{1,0:T(8,128)} %get-tuple-element.7.qg_ref, f32[384,1024]{1,0:T(8,128)} %get-tuple-element.8.refs_0_), custom_call_target="tpu_custom_call" | custom-call | tf_op jit(solution)/shard_map/apply/pallas_call | solution.py:349

commit v2 on v1

v2 whole, which is shorter than its diff:
```python
import functools

import jax
import jax.numpy as jnp
from jax import lax
from jax.experimental import pallas as pl
from jax.experimental.pallas import tpu as pltpu
from jax.sharding import PartitionSpec as P

LANES = 128
CHUNK = 2 * LANES
HIGH = lax.Precision.HIGH
F32 = jnp.float32
TREE_VMEM = 56 << 20
APPLY_VMEM = 56 << 20


def dot(a, b):
    return jnp.dot(a, b, precision=HIGH, preferred_element_type=F32)


def dot_nt(a, b):
    return lax.dot_general(
        a, b, (((1,), (1,)), ((), ())), precision=HIGH, preferred_element_type=F32
    )


def split(x):
    high = x.astype(jnp.bfloat16)
    return high, (x - high.astype(F32)).astype(jnp.bfloat16)


def level_order(bits, levels):
    return [bits - 1 - s for s in range(bits)] + list(range(bits, levels))


def local_offset(level, bits, rank):
    return rank * (2 ** (level - bits + 1) - 2)


def dot3(a_high, a_low, b_high, b_low):
    def one(a, b):
        return jnp.dot(a, b, preferred_element_type=F32)

    return one(a_high, b_high) + one(a_high, b_low) + one(a_low, b_high)


def tree_kernel(bits, levels, blocks, right_hbm, leaf_hbm, vt_hbm, ut_hbm, cores_hbm, *refs):
    x_hbm, qg_hbm, uh_hbm, ul_hbm = refs[:4]
    rbuf, leaf, vt_ref, ut_ref, core_g, sem_in, sem_out = refs[4:11]
    r_high, r_low, a_high, a_low, m_high, m_low, u_high, u_low, ql_ref, q_first = refs[11:21]
    gram_out, gram_in, first_out, first_in, later_out, later_in, q_out = refs[21:28]
    gram_sem, first_sem, later_sem, q_sem = refs[28:32]
    local_levels = list(range(bits, levels))
    core_l = refs[32 : 32 + len(local_levels)]
    ch_refs = refs[32 + len(local_levels) :]

    me = lax.axis_index("rows")
    rank, rows_dev = vt_ref.shape[1:]
    chunks = rbuf.shape[0]
    lf = rows_dev // blocks
    half_id = lax.rem(me, 2)
    upper = half_id == 1
    order = level_order(bits, levels)

    def child(s):
        return lax.rem(me // 2**s, 2)

    def partner(s):
        return me + (1 - 2 * child(s)) * 2**s

    barrier = pltpu.get_barrier_semaphore()
    for s in range(bits):
        pl.semaphore_signal(
            barrier, inc=1, device_id={"rows": partner(s)}, device_id_type=pl.DeviceIdType.MESH
        )

    slots = {"in": 0, "out": 0}

    def move(src, dst, sems, kind):
        copy = pltpu.make_async_copy(src, dst, sems.at[slots[kind]])
        slots[kind] += 1
        copy.start()
        return copy

    factor_loads = [move(vt_hbm, vt_ref, sem_in, "in"), move(ut_hbm, ut_ref, sem_in, "in")]
    leaf_load = move(leaf_hbm, leaf, sem_in, "in")
    core_loads = []
    for n, level in enumerate(local_levels):
        count = 2 ** (level - bits)
        src = cores_hbm.at[pl.ds(2**level - 1 + me * count, count)]
        core_loads.append(move(src, core_l[n], sem_in, "in"))
    right_loads = [
        move(right_hbm.at[:, pl.ds(c * CHUNK, CHUNK)], rbuf.at[c], sem_in, "in")
        for c in range(chunks)
    ]
    core_g_loads = []
    for s in range(bits):
        src = cores_hbm.at[2 ** (bits - 1 - s) - 1 + me // 2 ** (s + 1)]
        core_g_loads.append(move(src, core_g.at[s], sem_in, "in"))

    sent, written = [], []

    def send(src, dst, sems, s):
        copy = pltpu.make_async_remote_copy(
            src_ref=src,
            dst_ref=dst,
            send_sem=sems.at[0],
            recv_sem=sems.at[1],
            device_id={"rows": partner(s)},
            device_id_type=pl.DeviceIdType.MESH,
        )
        copy.start()
        sent.append(copy)
        return copy

    for copy in factor_loads:
        copy.wait()
    gram_cols = gram_out.shape[2]
    u_rows = [ut_ref[bits - 1 - s] for s in range(bits - 1)]
    pad = gram_cols - rank * (bits - 1)
    if pad:
        u_rows.append(jnp.zeros((pad, rows_dev), F32))
    v_rows = [vt_ref[bits - 1 - s] for s in range(1, bits)]
    gram_out[0] = dot_nt(jnp.concatenate(v_rows, 0), jnp.concatenate(u_rows, 0))
    pl.semaphore_wait(barrier, bits)
    gram_copy = {0: send(gram_out.at[0], gram_in.at[0], gram_sem.at[0], 0)}

    vt_all = jnp.concatenate([vt_ref[level] for level in order], 0)
    for copy in core_loads:
        copy.wait()
    for n, level in enumerate(local_levels):
        count = 2 ** (level - bits)
        node = rows_dev // count
        half = node // 2
        zero = jnp.zeros((rank, half), F32)
        for k in range(count):
            base = k * node
            u_a = ut_ref[level, :, base : base + half]
            u_b = ut_ref[level, :, base + half : base + node]
            diag = jnp.concatenate(
                [jnp.concatenate([u_a, zero], 1), jnp.concatenate([zero, u_b], 1)], 0
            )
            gram = dot_nt(vt_all[: rank * level, base : base + node], diag)
            core = core_l[n][k]
            ch_refs[n][k, : 2 * rank] = core
            ch_refs[n][k, 2 * rank :] = dot(gram, core)
    leaf_load.wait()
    high, low = split(leaf[...])
    a_high[:, :lf] = high
    a_low[:, :lf] = low
    v_high, v_low = split(vt_all)
    for i in range(blocks):
        rows = slice(i * lf, (i + 1) * lf)
        high, low = split(
            dot3(v_high[:, rows], v_low[:, rows], a_high[rows, :lf], a_low[rows, :lf])
        )
        m_high[i] = high
        m_low[i] = low

    first_copy, later_copy, q_copy = {}, {}, {}

    def forward(c):
        right_loads[c].wait()
        high, low = split(rbuf[c])
        r_high[c] = high
        r_low[c] = low
        parts = []
        for i in range(blocks):
            rows = slice(i * lf, (i + 1) * lf)
            parts.append(dot3(m_high[i], m_low[i], r_high[c, rows, :], r_low[c, rows, :]))
        for n in reversed(range(len(local_levels))):
            level = local_levels[n]
            top = rank * level
            merged = []
            for k in range(len(parts) // 2):
                a, b = parts[2 * k], parts[2 * k + 1]
                image = dot(ch_refs[n][k], jnp.concatenate([b[top:], a[top:]], 0))
                start = local_offset(level, bits, rank) + 2 * rank * k
                ql_ref[c, start : start + 2 * rank] = image[: 2 * rank]
                merged.append(a[:top] + b[:top] - image[2 * rank :])
            parts = merged
        p = parts[0]
        low, high = p[:, :LANES], p[:, LANES:]
        first_out[c, :rank] = low[:rank]
        first_out[c, rank : 2 * rank] = high[:rank]
        first_out[c, 2 * rank :] = jnp.where(upper, low[rank:], high[rank:])
        first_copy[c] = send(first_out.at[c], first_in.at[c], first_sem.at[c], 0)
        later_out[0, c] = jnp.where(upper, high[rank:], low[rank:])

    def bases():
        if local_levels:
            rows = [ut_ref[level] for level in local_levels]
            extra = a_high.shape[1] - lf - rank * len(rows)
            if extra:
                rows.append(jnp.zeros((extra, rows_dev), F32))
            high, low = split(-jnp.concatenate(rows, 0).T)
            a_high[:, lf:] = high
            a_low[:, lf:] = low
        rows = [ut_ref[bits - 1 - s] for s in range(bits)]
        extra = u_high.shape[1] - rank * bits
        if extra:
            rows.append(jnp.zeros((extra, rows_dev), F32))
        high, low = split(-jnp.concatenate(rows, 0).T)
        u_high[...] = high
        u_low[...] = low
        written.append(move(u_high, uh_hbm, sem_out, "out"))
        written.append(move(u_low, ul_hbm, sem_out, "out"))

    def leaves(c):
        for i in range(blocks):
            rows = slice(i * lf, (i + 1) * lf)
            highs, lows = [r_high[c, rows, :]], [r_low[c, rows, :]]
            width = lf
            for level in local_levels:
                place = rank * (i * 2 ** (level - bits + 1) // blocks)
                start = local_offset(level, bits, rank) + place
                high, low = split(ql_ref[c, start : start + rank])
                highs.append(high)
                lows.append(low)
                width += rank
            if a_high.shape[1] > width:
                zero = jnp.zeros((a_high.shape[1] - width, CHUNK), jnp.bfloat16)
                highs.append(zero)
                lows.append(zero)
            rbuf[c, rows, :] = dot3(
                a_high[rows, :],
                a_low[rows, :],
                jnp.concatenate(highs, 0),
                jnp.concatenate(lows, 0),
            )
        written.append(move(rbuf.at[c], x_hbm.at[:, pl.ds(c * CHUNK, CHUNK)], sem_out, "out"))

    def stack(mine, theirs, s):
        first = child(s) == 0
        return jnp.concatenate([jnp.where(first, theirs, mine), jnp.where(first, mine, theirs)], 0)

    def pick(image, s):
        first = child(s) == 0
        return (
            jnp.where(first, image[:rank], image[rank:]),
            jnp.where(first, image[rank:], image[:rank]),
        )

    def correction(s, own, sib):
        zeros = [jnp.zeros((rank, LANES), F32)]
        before, after = s, gram_cols // rank - 1 - s
        rows = slice(rank * s, None)
        q_own = jnp.concatenate(zeros * before + [own] + zeros * after, 0)
        q_sib = jnp.concatenate(zeros * before + [sib] + zeros * after, 0)
        return dot(gram_out[s, rows, :], q_own) + dot(gram_in[s, rows, :], q_sib)

    def grams(s):
        gram_copy[s].wait_recv()
        if s + 1 < bits - 1:
            gram_out[s + 1] = gram_out[s] + gram_in[s]
            gram_copy[s + 1] = send(
                gram_out.at[s + 1], gram_in.at[s + 1], gram_sem.at[s + 1], s + 1
            )

    def step(s, c):
        if c == 0:
            core_g_loads[s].wait()
        if s == 0:
            first_copy[c].wait_recv()
            mine = jnp.concatenate([first_out[c, :rank], first_out[c, rank : 2 * rank]], 1)
            theirs = jnp.concatenate([first_in[c, :rank], first_in[c, rank : 2 * rank]], 1)
            image = dot(core_g[0], stack(mine, theirs, 0))
            own, sib = pick(image, 0)
            q_first[c] = own
            own = jnp.where(upper, own[:, LANES:], own[:, :LANES])
            sib = jnp.where(upper, sib[:, LANES:], sib[:, :LANES])
            rest = later_out[0, c] + first_in[c, 2 * rank :]
        else:
            later_copy[s, c].wait_recv()
            live = slice(rank * (s - 1), rank * s)
            image = dot(core_g[s], stack(later_out[s, c, live], later_in[s, c, live], s))
            own, sib = pick(image, s)
            q_out[s - 1, c] = own
            start = pl.multiple_of(c * CHUNK + half_id * LANES, LANES)
            target = qg_hbm.at[pl.ds(s * rank, rank), pl.ds(start, LANES)]
            q_copy[s, c] = send(q_out.at[s - 1, c], target, q_sem.at[s - 1, c], 0)
            if s < bits - 1:
                rest = later_out[s, c, rank * s :] + later_in[s, c, rank * s :]
        if s < bits - 1:
            later_out[s + 1, c, rank * s :] = rest - correction(s, own, sib)
            later_copy[s + 1, c] = send(
                later_out.at[s + 1, c, pl.ds(rank * s, rank * (bits - 1 - s))],
                later_in.at[s + 1, c, pl.ds(rank * s, rank * (bits - 1 - s))],
                later_sem.at[s, c],
                s + 1,
            )
        if s == 0:
            target = qg_hbm.at[pl.ds(0, rank), pl.ds(c * CHUNK, CHUNK)]
            written.append(move(q_first.at[c], target, sem_out, "out"))
        else:
            written.append(move(q_out.at[s - 1, c], target, sem_out, "out"))

    for c in range(chunks):
        forward(c)
        if c == 0:
            grams(0)
    for s in range(1, bits - 1):
        grams(s)
    bases()
    for t in range(chunks + bits - 1):
        for s in range(bits):
            c = t - s
            if 0 <= c < chunks:
                step(s, c)
        if t < chunks:
            leaves(t)
    for copy in q_copy.values():
        copy.wait_recv()
    for copy in written:
        copy.wait()
    for copy in sent:
        copy.wait_send()


def tree(bits, right_side, leaf_inverse, vt, ut, cores):
    rows_dev, cols = right_side.shape
    lf = leaf_inverse.shape[1]
    levels, rank = vt.shape[:2]
    blocks = rows_dev // lf
    chunks = cols // CHUNK
    local_levels = list(range(bits, levels))
    assert blocks == 2 ** len(local_levels) and bits >= 2
    gram_cols = pl.cdiv(rank * (bits - 1), LANES) * LANES
    depth = lf + pl.cdiv(rank * len(local_levels), LANES) * LANES
    wide = pl.cdiv(rank * bits, LANES) * LANES
    out_shape = [
        jax.ShapeDtypeStruct((rows_dev, cols), F32),
        jax.ShapeDtypeStruct((rank * bits, cols), F32),
        jax.ShapeDtypeStruct((rows_dev, wide), jnp.bfloat16),
        jax.ShapeDtypeStruct((rows_dev, wide), jnp.bfloat16),
    ]
    hbm = pl.BlockSpec(memory_space=pl.ANY)
    counts = [2 ** (level - bits) for level in local_levels]
    rest = rank * (bits - 1)
    half = jnp.bfloat16
    scratch = [
        pltpu.VMEM((chunks, rows_dev, CHUNK), F32),
        pltpu.VMEM((rows_dev, lf), F32),
        pltpu.VMEM((levels, rank, rows_dev), F32),
        pltpu.VMEM((levels, rank, rows_dev), F32),
        pltpu.VMEM((bits, 2 * rank, 2 * rank), F32),
        pltpu.SemaphoreType.DMA((3 + levels + chunks,)),
        pltpu.SemaphoreType.DMA((2 + chunks * (bits + 1),)),
        pltpu.VMEM((chunks, rows_dev, CHUNK), half),
        pltpu.VMEM((chunks, rows_dev, CHUNK), half),
        pltpu.VMEM((rows_dev, depth), half),
        pltpu.VMEM((rows_dev, depth), half),
        pltpu.VMEM((blocks, levels * rank, lf), half),
        pltpu.VMEM((blocks, levels * rank, lf), half),
        pltpu.VMEM((rows_dev, wide), half),
        pltpu.VMEM((rows_dev, wide), half),
        pltpu.VMEM((chunks, max(rank * (2 * blocks - 2), rank), CHUNK), F32),
        pltpu.VMEM((chunks, rank, CHUNK), F32),
        pltpu.VMEM((bits - 1, rest, gram_cols), F32),
        pltpu.VMEM((bits - 1, rest, gram_cols), F32),
        pltpu.VMEM((chunks, 2 * rank + rest, LANES), F32),
        pltpu.VMEM((chunks, 2 * rank + rest, LANES), F32),
        pltpu.VMEM((bits, chunks, rest, LANES), F32),
        pltpu.VMEM((bits, chunks, rest, LANES), F32),
        pltpu.VMEM((bits - 1, chunks, rank, LANES), F32),
        pltpu.SemaphoreType.DMA((bits - 1, 2)),
        pltpu.SemaphoreType.DMA((chunks, 2)),
        pltpu.SemaphoreType.DMA((bits - 1, chunks, 2)),
        pltpu.SemaphoreType.DMA((bits - 1, chunks, 2)),
    ]
    scratch += [pltpu.VMEM((count, 2 * rank, 2 * rank), F32) for count in counts]
    scratch += [
        pltpu.VMEM((count, rank * (level + 2), 2 * rank), F32)
        for count, level in zip(counts, local_levels)
    ]
    return pl.pallas_call(
        functools.partial(tree_kernel, bits, levels, blocks),
        out_shape=out_shape,
        in_specs=[hbm] * 5,
        out_specs=[hbm] * 4,
        scratch_shapes=scratch,
        compiler_params=pltpu.CompilerParams(
            collective_id=0, has_side_effects=True, vmem_limit_bytes=TREE_VMEM
        ),
        name="tree",
    )(right_side, leaf_inverse, vt, ut, cores)


def apply_kernel(x_ref, uh_ref, ul_ref, q_ref, out_ref):
    pad = uh_ref.shape[1] - q_ref.shape[0]
    q = q_ref[...]
    if pad:
        q = jnp.concatenate([q, jnp.zeros((pad, q.shape[1]), F32)], 0)
    high, low = split(q)
    out_ref[...] = x_ref[...] + dot3(uh_ref[...], ul_ref[...], high, low)


def apply(x, q, u_high, u_low):
    rows_dev, cols = x.shape
    width = CHUNK

    def column(rows):
        return pl.BlockSpec((rows, width), lambda c: (0, c))

    whole = pl.BlockSpec(u_high.shape, lambda c: (0, 0))
    return pl.pallas_call(
        apply_kernel,
        grid=(cols // width,),
        out_shape=jax.ShapeDtypeStruct((rows_dev, cols), F32),
        in_specs=[column(rows_dev), whole, whole, column(q.shape[0])],
        out_specs=column(rows_dev),
        compiler_params=pltpu.CompilerParams(vmem_limit_bytes=APPLY_VMEM),
        name="apply",
    )(x, u_high, u_low, q)


def local(bits, right_side, leaf_inverse, left_factors, right_factors, cores):
    ut = jnp.swapaxes(left_factors, 1, 2)
    vt = jnp.swapaxes(right_factors, 1, 2)
    x, q, u_high, u_low = tree(bits, right_side, leaf_inverse, vt, ut, cores)
    return apply(x, q, u_high, u_low)


def solution(mesh):
    bits = mesh.shape["rows"].bit_length() - 1
    in_specs = (
        P(("rep", "rows"), None),
        P(("rep", "rows"), None),
        P(None, ("rep", "rows"), None),
        P(None, ("rep", "rows"), None),
        P("rep", None, None),
    )
    out_specs = P(("rep", "rows"), None)
    return jax.shard_map(
        functools.partial(local, bits),
        mesh=mesh,
        in_specs=in_specs,
        out_specs=out_specs,
        check_vma=False,
    )
```

time: 49.2 us -> 41.5 us (0.84)
  Pallas kernels: 48.9 us -> 41.4 us
    pallas_call x1, Pallas kernels: 38.9 us -> 35 us  [tree(): pl.pallas_call(functools.partial(tree_kernel, bits, levels, blocks), out_...]
    pallas_call x1, Pallas kernels: 10.1 us -> 6.35 us  [apply(): pl.pallas_call(apply_kernel, grid=(cols // width,), out_shape=jax.ShapeDt...]
where the time goes in v2:
time: 41.5 us; the launch traced here: 41.4 us
  Pallas kernels  41.4 us (100%)
    pallas_call x1, Pallas kernels, tree(): pl.pallas_call(functools.partial(tree_kernel, bits, levels, blocks), out_...  35 us
    pallas_call x1, Pallas kernels, apply(): pl.pallas_call(apply_kernel, grid=(cols // width,), out_shape=jax.ShapeDt...  6.35 us

profile of v2, /device:TPU:0, one launch (start us, length us, event | category | flops | bytes accessed | tf_op | source)
XLA Modules:
  0.0 41.4 jit_solution(12512975039198771253)
XLA Ops:
  0.0 35.0 %tree.1 = (f32[1024,1024]{1,0:T(8,128)}, f32[192,1024]{1,0:T(8,128)}, bf16[1024,256]{1,0:T(8,128)(2,1)}, bf16[1024,256]{1,0:T(8,128)(2,1)}) custom-call(f32[1024,1024]{1,0:T(8,128)} %right_hbm.1, f32[1024,256]{1,0:T(8,128)} %leaf_hbm.1, f32[5,64,1024]{2,1,0:T(8,128)} %bitcast.2, f32[5,64,1024]{2,1,0:T(8,128)} %bitcast.3, f32[31,128,128]{2,1,0:T(8,128)} %cores_hbm.1), custom_call_target="tpu_custom_call" | custom-call | tf_op jit(solution)/shard_map/tree/pallas_call | solution.py:377
  35.0 6.4 %apply.1 = f32[1024,1024]{1,0:T(8,128)} custom-call(f32[1024,1024]{1,0:T(8,128)} %get-tuple-element.9.x_ref, bf16[1024,256]{1,0:T(8,128)(2,1)} %get-tuple-element.10.uh_ref, bf16[1024,256]{1,0:T(8,128)(2,1)} %get-tuple-element.11.ul_ref, f32[192,1024]{1,0:T(8,128)} %get-tuple-element.12.q_ref), custom_call_target="tpu_custom_call" | custom-call | tf_op jit(solution)/shard_map/apply/pallas_call | solution.py:407

commit v3 on v2

--- a/solution.py
+++ b/solution.py
@@ -9,20 +9,9 @@
 
 LANES = 128
 CHUNK = 2 * LANES
-HIGH = lax.Precision.HIGH
 F32 = jnp.float32
-TREE_VMEM = 56 << 20
-APPLY_VMEM = 56 << 20
-
-
-def dot(a, b):
-    return jnp.dot(a, b, precision=HIGH, preferred_element_type=F32)
-
-
-def dot_nt(a, b):
-    return lax.dot_general(
-        a, b, (((1,), (1,)), ((), ())), precision=HIGH, preferred_element_type=F32
-    )
+TREE_VMEM = 24 << 20
+APPLY_VMEM = 12 << 20
 
 
 def split(x):
@@ -38,11 +27,17 @@
     return rank * (2 ** (level - bits + 1) - 2)
 
 
-def dot3(a_high, a_low, b_high, b_low):
-    def one(a, b):
-        return jnp.dot(a, b, preferred_element_type=F32)
-
-    return one(a_high, b_high) + one(a_high, b_low) + one(a_low, b_high)
+def dot3(a, b, nt=False):
+    dims = (((1,), (1 if nt else 0,)), ((), ()))
+
+    def one(x, y):
+        return lax.dot_general(x, y, dims, preferred_element_type=F32)
+
+    return one(a[0], b[0]) + one(a[0], b[1]) + one(a[1], b[0])
+
+
+def dot(a, b):
+    return dot3(split(a), split(b))
 
 
 def tree_kernel(bits, levels, blocks, right_hbm, leaf_hbm, vt_hbm, ut_hbm, cores_hbm, *refs):
@@ -54,6 +49,7 @@
     local_levels = list(range(bits, levels))
     core_l = refs[32 : 32 + len(local_levels)]
     ch_refs = refs[32 + len(local_levels) :]
+    ch_refs = list(zip(ch_refs[::2], ch_refs[1::2]))
 
     me = lax.axis_index("rows")
     rank, rows_dev = vt_ref.shape[1:]
@@ -117,43 +113,47 @@
     for copy in factor_loads:
         copy.wait()
     gram_cols = gram_out.shape[2]
-    u_rows = [ut_ref[bits - 1 - s] for s in range(bits - 1)]
-    pad = gram_cols - rank * (bits - 1)
-    if pad:
-        u_rows.append(jnp.zeros((pad, rows_dev), F32))
-    v_rows = [vt_ref[bits - 1 - s] for s in range(1, bits)]
-    gram_out[0] = dot_nt(jnp.concatenate(v_rows, 0), jnp.concatenate(u_rows, 0))
+    vt = split(jnp.concatenate([vt_ref[level] for level in order], 0))
+    ut = split(jnp.concatenate([ut_ref[level] for level in order], 0))
+    v_rows = [v[rank : rank * bits] for v in vt]
+    u_rows = [u[:gram_cols] for u in ut]
+    gram_out[0] = dot3(v_rows, u_rows, nt=True)
     pl.semaphore_wait(barrier, bits)
     gram_copy = {0: send(gram_out.at[0], gram_in.at[0], gram_sem.at[0], 0)}
 
-    vt_all = jnp.concatenate([vt_ref[level] for level in order], 0)
     for copy in core_loads:
         copy.wait()
     for n, level in enumerate(local_levels):
         count = 2 ** (level - bits)
         node = rows_dev // count
         half = node // 2
-        zero = jnp.zeros((rank, half), F32)
+        zero = jnp.zeros((rank, half), jnp.bfloat16)
+        own = slice(rank * level, rank * (level + 1))
         for k in range(count):
             base = k * node
-            u_a = ut_ref[level, :, base : base + half]
-            u_b = ut_ref[level, :, base + half : base + node]
-            diag = jnp.concatenate(
-                [jnp.concatenate([u_a, zero], 1), jnp.concatenate([zero, u_b], 1)], 0
-            )
-            gram = dot_nt(vt_all[: rank * level, base : base + node], diag)
+            diag = [
+                jnp.concatenate(
+                    [
+                        jnp.concatenate([u[own, base : base + half], zero], 1),
+                        jnp.concatenate([zero, u[own, base + half : base + node]], 1),
+                    ],
+                    0,
+                )
+                for u in ut
+            ]
+            gram = dot3([v[: rank * level, base : base + node] for v in vt], diag, nt=True)
             core = core_l[n][k]
-            ch_refs[n][k, : 2 * rank] = core
-            ch_refs[n][k, 2 * rank :] = dot(gram, core)
+            for ref, top, rest in zip(ch_refs[n], split(core), split(dot(gram, core))):
+                ref[k, : 2 * rank] = top
+                ref[k, 2 * rank :] = rest
     leaf_load.wait()
     high, low = split(leaf[...])
     a_high[:, :lf] = high
     a_low[:, :lf] = low
-    v_high, v_low = split(vt_all)
     for i in range(blocks):
         rows = slice(i * lf, (i + 1) * lf)
         high, low = split(
-            dot3(v_high[:, rows], v_low[:, rows], a_high[rows, :lf], a_low[rows, :lf])
+            dot3([v[:, rows] for v in vt], (a_high[rows, :lf], a_low[rows, :lf]))
         )
         m_high[i] = high
         m_low[i] = low
@@ -168,14 +168,15 @@
         parts = []
         for i in range(blocks):
             rows = slice(i * lf, (i + 1) * lf)
-            parts.append(dot3(m_high[i], m_low[i], r_high[c, rows, :], r_low[c, rows, :]))
+            parts.append(dot3((m_high[i], m_low[i]), (r_high[c, rows, :], r_low[c, rows, :])))
         for n in reversed(range(len(local_levels))):
             level = local_levels[n]
             top = rank * level
             merged = []
             for k in range(len(parts) // 2):
                 a, b = parts[2 * k], parts[2 * k + 1]
-                image = dot(ch_refs[n][k], jnp.concatenate([b[top:], a[top:]], 0))
+                both = jnp.concatenate([b[top:], a[top:]], 0)
+                image = dot3((ch_refs[n][0][k], ch_refs[n][1][k]), split(both))
                 start = local_offset(level, bits, rank) + 2 * rank * k
                 ql_ref[c, start : start + 2 * rank] = image[: 2 * rank]
                 merged.append(a[:top] + b[:top] - image[2 * rank :])
@@ -224,10 +225,8 @@
                 highs.append(zero)
                 lows.append(zero)
             rbuf[c, rows, :] = dot3(
-                a_high[rows, :],
-                a_low[rows, :],
-                jnp.concatenate(highs, 0),
-                jnp.concatenate(lows, 0),
+                (a_high[rows, :], a_low[rows, :]),
+                (jnp.concatenate(highs, 0), jnp.concatenate(lows, 0)),
             )
         written.append(move(rbuf.at[c], x_hbm.at[:, pl.ds(c * CHUNK, CHUNK)], sem_out, "out"))
 
@@ -335,7 +334,8 @@
         jax.ShapeDtypeStruct((rows_dev, wide), jnp.bfloat16),
         jax.ShapeDtypeStruct((rows_dev, wide), jnp.bfloat16),
     ]
-    hbm = pl.BlockSpec(memory_space=pl.ANY)
+    hbm = pl.BlockSpec(memory_space=pltpu.HBM)
+    free = pl.BlockSpec(memory_space=pl.ANY)
     counts = [2 ** (level - bits) for level in local_levels]
     rest = rank * (bits - 1)
     half = jnp.bfloat16
@@ -371,17 +371,18 @@
     ]
     scratch += [pltpu.VMEM((count, 2 * rank, 2 * rank), F32) for count in counts]
     scratch += [
-        pltpu.VMEM((count, rank * (level + 2), 2 * rank), F32)
+        pltpu.VMEM((count, rank * (level + 2), 2 * rank), half)
         for count, level in zip(counts, local_levels)
+        for _ in range(2)
     ]
     return pl.pallas_call(
         functools.partial(tree_kernel, bits, levels, blocks),
         out_shape=out_shape,
         in_specs=[hbm] * 5,
-        out_specs=[hbm] * 4,
+        out_specs=[free] * 4,
         scratch_shapes=scratch,
         compiler_params=pltpu.CompilerParams(
-            collective_id=0, has_side_effects=True, vmem_limit_bytes=TREE_VMEM
+            collective_id=0, has_side_effects=True, vmem_limit_bytes=TREE_VMEM + 32 * rows_dev * lf
         ),
         name="tree",
     )(right_side, leaf_inverse, vt, ut, cores)
@@ -393,7 +394,7 @@
     if pad:
         q = jnp.concatenate([q, jnp.zeros((pad, q.shape[1]), F32)], 0)
     high, low = split(q)
-    out_ref[...] = x_ref[...] + dot3(uh_ref[...], ul_ref[...], high, low)
+    out_ref[...] = x_ref[...] + dot3((uh_ref[...], ul_ref[...]), (high, low))
 
 
 def apply(x, q, u_high, u_low):
@@ -418,6 +419,10 @@
 def local(bits, right_side, leaf_inverse, left_factors, right_factors, cores):
     ut = jnp.swapaxes(left_factors, 1, 2)
     vt = jnp.swapaxes(right_factors, 1, 2)
+    right_side, leaf_inverse, vt, ut, cores = (
+        pltpu.with_memory_space_constraint(a, pltpu.HBM)
+        for a in (right_side, leaf_inverse, vt, ut, cores)
+    )
     x, q, u_high, u_low = tree(bits, right_side, leaf_inverse, vt, ut, cores)
     return apply(x, q, u_high, u_low)
 

time: 41.5 us -> 39.2 us (0.945)
  Pallas kernels: 41.4 us -> 39 us
    pallas_call x1, Pallas kernels: 6.35 us -> 3.99 us  [apply(): pl.pallas_call(apply_kernel, grid=(cols // width,), out_shape=jax.ShapeDt...]
where the time goes in v3:
time: 39.2 us; the launch traced here: 39.1 us
  Pallas kernels  39 us (99%)
    pallas_call x1, Pallas kernels, tree(): pl.pallas_call(functools.partial(tree_kernel, bits, levels, blocks), out_...  35.1 us
    pallas_call x1, Pallas kernels, apply(): pl.pallas_call(apply_kernel, grid=(cols // width,), out_shape=jax.ShapeDt...  3.99 us

profile of v3, /device:TPU:0, one launch (start us, length us, event | category | flops | bytes accessed | tf_op | source)
XLA Modules:
  0.0 39.1 jit_solution(17173365833234874060)
XLA Ops:
  0.0 35.1 %tree.1 = (f32[1024,1024]{1,0:T(8,128)S(1)}, f32[192,1024]{1,0:T(8,128)S(1)}, bf16[1024,256]{1,0:T(8,128)(2,1)S(1)}, bf16[1024,256]{1,0:T(8,128)(2,1)S(1)}) custom-call(f32[1024,1024]{1,0:T(8,128)} %right_hbm.1, f32[1024,256]{1,0:T(8,128)} %leaf_hbm.1, f32[5,64,1024]{2,1,0:T(8,128)} %bitcast.2, f32[5,64,1024]{2,1,0:T(8,128)} %bitcast.3, ...), custom_call_target="tpu_custom_call" | custom-call | tf_op jit(solution)/shard_map/tree/pallas_call | solution.py:378
  35.1 4.0 %apply.1 = f32[1024,1024]{1,0:T(8,128)} custom-call(f32[1024,1024]{1,0:T(8,128)S(1)} %get-tuple-element.9.x_ref, bf16[1024,256]{1,0:T(8,128)(2,1)S(1)} %get-tuple-element.10.uh_ref, bf16[1024,256]{1,0:T(8,128)(2,1)S(1)} %get-tuple-element.11.ul_ref, f32[192,1024]{1,0:T(8,128)S(1)} %get-tuple-element.12.q_ref), custom_call_target="tpu_custom_call" | custom-call | tf_op jit(solution)/shard_map/apply/pallas_call | solution.py:408

commit v4 on v3

--- a/solution.py
+++ b/solution.py
@@ -46,9 +46,10 @@
     r_high, r_low, a_high, a_low, m_high, m_low, u_high, u_low, ql_ref, q_first = refs[11:21]
     gram_out, gram_in, first_out, first_in, later_out, later_in, q_out = refs[21:28]
     gram_sem, first_sem, later_sem, q_sem = refs[28:32]
+    last_in, last_q, last_sem = refs[32:35]
     local_levels = list(range(bits, levels))
-    core_l = refs[32 : 32 + len(local_levels)]
-    ch_refs = refs[32 + len(local_levels) :]
+    core_l = refs[35 : 35 + len(local_levels)]
+    ch_refs = refs[35 + len(local_levels) :]
     ch_refs = list(zip(ch_refs[::2], ch_refs[1::2]))
 
     me = lax.axis_index("rows")
@@ -65,10 +66,11 @@
     def partner(s):
         return me + (1 - 2 * child(s)) * 2**s
 
+    cross = partner(bits - 1) + (1 - 2 * child(0))
     barrier = pltpu.get_barrier_semaphore()
-    for s in range(bits):
+    for target in [partner(s) for s in range(bits)] + [cross]:
         pl.semaphore_signal(
-            barrier, inc=1, device_id={"rows": partner(s)}, device_id_type=pl.DeviceIdType.MESH
+            barrier, inc=1, device_id={"rows": target}, device_id_type=pl.DeviceIdType.MESH
         )
 
     slots = {"in": 0, "out": 0}
@@ -97,13 +99,13 @@
 
     sent, written = [], []
 
-    def send(src, dst, sems, s):
+    def send(src, dst, sems, s, target=None):
         copy = pltpu.make_async_remote_copy(
             src_ref=src,
             dst_ref=dst,
             send_sem=sems.at[0],
             recv_sem=sems.at[1],
-            device_id={"rows": partner(s)},
+            device_id={"rows": partner(s) if target is None else target},
             device_id_type=pl.DeviceIdType.MESH,
         )
         copy.start()
@@ -118,7 +120,7 @@
     v_rows = [v[rank : rank * bits] for v in vt]
     u_rows = [u[:gram_cols] for u in ut]
     gram_out[0] = dot3(v_rows, u_rows, nt=True)
-    pl.semaphore_wait(barrier, bits)
+    pl.semaphore_wait(barrier, bits + 1)
     gram_copy = {0: send(gram_out.at[0], gram_in.at[0], gram_sem.at[0], 0)}
 
     for copy in core_loads:
@@ -158,7 +160,7 @@
         m_high[i] = high
         m_low[i] = low
 
-    first_copy, later_copy, q_copy = {}, {}, {}
+    first_copy, later_copy, q_copy, last_copy = {}, {}, {}, {}
 
     def forward(c):
         right_loads[c].wait()
@@ -257,9 +259,29 @@
                 gram_out.at[s + 1], gram_in.at[s + 1], gram_sem.at[s + 1], s + 1
             )
 
+    def last_step(s, c):
+        later_copy[s, c].wait_recv()
+        last_copy[0].wait_recv()
+        last_copy[1].wait_recv()
+        live = slice(rank * (s - 1), rank * s)
+
+        def join(here, there):
+            return jnp.concatenate(
+                [jnp.where(upper, there, here), jnp.where(upper, here, there)], 1
+            )
+
+        mine = join(later_out[s, c, live], last_in[0])
+        theirs = join(later_in[s, c, live], last_in[1])
+        last_q[...] = pick(dot(core_g[s], stack(mine, theirs, s)), s)[0]
+        target = qg_hbm.at[pl.ds(s * rank, rank), pl.ds(c * CHUNK, CHUNK)]
+        written.append(move(last_q, target, sem_out, "out"))
+
     def step(s, c):
         if c == 0:
             core_g_loads[s].wait()
+        if s == bits - 1 and c == chunks - 1:
+            last_step(s, c)
+            return
         if s == 0:
             first_copy[c].wait_recv()
             mine = jnp.concatenate([first_out[c, :rank], first_out[c, rank : 2 * rank]], 1)
@@ -283,6 +305,10 @@
                 rest = later_out[s, c, rank * s :] + later_in[s, c, rank * s :]
         if s < bits - 1:
             later_out[s + 1, c, rank * s :] = rest - correction(s, own, sib)
+            if s == bits - 2 and c == chunks - 1:
+                root = later_out.at[s + 1, c, pl.ds(rank * s, rank)]
+                last_copy[1] = send(root, last_in.at[1], last_sem.at[1], None, cross)
+                last_copy[0] = send(root, last_in.at[0], last_sem.at[0], 0)
             later_copy[s + 1, c] = send(
                 later_out.at[s + 1, c, pl.ds(rank * s, rank * (bits - 1 - s))],
                 later_in.at[s + 1, c, pl.ds(rank * s, rank * (bits - 1 - s))],
@@ -368,6 +394,9 @@
         pltpu.SemaphoreType.DMA((chunks, 2)),
         pltpu.SemaphoreType.DMA((bits - 1, chunks, 2)),
         pltpu.SemaphoreType.DMA((bits - 1, chunks, 2)),
+        pltpu.VMEM((2, rank, LANES), F32),
+        pltpu.VMEM((rank, CHUNK), F32),
+        pltpu.SemaphoreType.DMA((2, 2)),
     ]
     scratch += [pltpu.VMEM((count, 2 * rank, 2 * rank), F32) for count in counts]
     scratch += [

time: 39.2 us -> 38.3 us (0.977)
  Pallas kernels: 39 us -> 38.2 us
    pallas_call x1, Pallas kernels: 35.1 us -> 34.2 us  [tree(): pl.pallas_call(functools.partial(tree_kernel, bits, levels, blocks), out_...]
where the time goes in v4:
time: 38.3 us; the launch traced here: 38.2 us
  Pallas kernels  38.2 us (100%)
    pallas_call x1, Pallas kernels, tree(): pl.pallas_call(functools.partial(tree_kernel, bits, levels, blocks), out_...  34.2 us
    pallas_call x1, Pallas kernels, apply(): pl.pallas_call(apply_kernel, grid=(cols // width,), out_shape=jax.ShapeDt...  3.99 us

profile of v4, /device:TPU:0, one launch (start us, length us, event | category | flops | bytes accessed | tf_op | source)
XLA Modules:
  0.0 38.2 jit_solution(1445979513392035875)
XLA Ops:
  0.0 34.2 %tree.1 = (f32[1024,1024]{1,0:T(8,128)S(1)}, f32[192,1024]{1,0:T(8,128)S(1)}, bf16[1024,256]{1,0:T(8,128)(2,1)S(1)}, bf16[1024,256]{1,0:T(8,128)(2,1)S(1)}) custom-call(f32[1024,1024]{1,0:T(8,128)} %right_hbm.1, f32[1024,256]{1,0:T(8,128)} %leaf_hbm.1, f32[5,64,1024]{2,1,0:T(8,128)} %bitcast.2, f32[5,64,1024]{2,1,0:T(8,128)} %bitcast.3, ...), custom_call_target="tpu_custom_call" | custom-call | tf_op jit(solution)/shard_map/tree/pallas_call | solution.py:407
  34.2 4.0 %apply.1 = f32[1024,1024]{1,0:T(8,128)} custom-call(f32[1024,1024]{1,0:T(8,128)S(1)} %get-tuple-element.9.x_ref, bf16[1024,256]{1,0:T(8,128)(2,1)S(1)} %get-tuple-element.10.uh_ref, bf16[1024,256]{1,0:T(8,128)(2,1)S(1)} %get-tuple-element.11.ul_ref, f32[192,1024]{1,0:T(8,128)S(1)} %get-tuple-element.12.q_ref), custom_call_target="tpu_custom_call" | custom-call | tf_op jit(solution)/shard_map/apply/pallas_call | solution.py:437

commit v5 on v4

--- a/solution.py
+++ b/solution.py
@@ -167,7 +167,7 @@
         high, low = split(rbuf[c])
         r_high[c] = high
         r_low[c] = low
-        parts = []
+        parts, later = [], []
         for i in range(blocks):
             rows = slice(i * lf, (i + 1) * lf)
             parts.append(dot3((m_high[i], m_low[i]), (r_high[c, rows, :], r_low[c, rows, :])))
@@ -177,11 +177,11 @@
             merged = []
             for k in range(len(parts) // 2):
                 a, b = parts[2 * k], parts[2 * k + 1]
-                both = jnp.concatenate([b[top:], a[top:]], 0)
-                image = dot3((ch_refs[n][0][k], ch_refs[n][1][k]), split(both))
+                both = split(jnp.concatenate([b[top:], a[top:]], 0))
+                change = dot3([ref[k, 2 * rank :] for ref in ch_refs[n]], both)
                 start = local_offset(level, bits, rank) + 2 * rank * k
-                ql_ref[c, start : start + 2 * rank] = image[: 2 * rank]
-                merged.append(a[:top] + b[:top] - image[2 * rank :])
+                later.append((start, n, k, both))
+                merged.append(a[:top] + b[:top] - change)
             parts = merged
         p = parts[0]
         low, high = p[:, :LANES], p[:, LANES:]
@@ -190,6 +190,10 @@
         first_out[c, 2 * rank :] = jnp.where(upper, low[rank:], high[rank:])
         first_copy[c] = send(first_out.at[c], first_in.at[c], first_sem.at[c], 0)
         later_out[0, c] = jnp.where(upper, high[rank:], low[rank:])
+        for start, n, k, both in later:
+            ql_ref[c, start : start + 2 * rank] = dot3(
+                [ref[k, : 2 * rank] for ref in ch_refs[n]], both
+            )
 
     def bases():
         if local_levels:

time: 38.3 us -> 37.6 us (0.982)
  Pallas kernels: 38.2 us -> 37.5 us
    pallas_call x1, Pallas kernels: 34.2 us -> 33.5 us  [tree(): pl.pallas_call(functools.partial(tree_kernel, bits, levels, blocks), out_...]
where the time goes in v5:
time: 37.6 us; the launch traced here: 37.5 us
  Pallas kernels  37.5 us (100%)
    pallas_call x1, Pallas kernels, tree(): pl.pallas_call(functools.partial(tree_kernel, bits, levels, blocks), out_...  33.5 us
    pallas_call x1, Pallas kernels, apply(): pl.pallas_call(apply_kernel, grid=(cols // width,), out_shape=jax.ShapeDt...  3.99 us

profile of v5, /device:TPU:0, one launch (start us, length us, event | category | flops | bytes accessed | tf_op | source)
XLA Modules:
  0.0 37.5 jit_solution(11620274225088377839)
XLA Ops:
  0.0 33.5 %tree.1 = (f32[1024,1024]{1,0:T(8,128)S(1)}, f32[192,1024]{1,0:T(8,128)S(1)}, bf16[1024,256]{1,0:T(8,128)(2,1)S(1)}, bf16[1024,256]{1,0:T(8,128)(2,1)S(1)}) custom-call(f32[1024,1024]{1,0:T(8,128)} %right_hbm.1, f32[1024,256]{1,0:T(8,128)} %leaf_hbm.1, f32[5,64,1024]{2,1,0:T(8,128)} %bitcast.2, f32[5,64,1024]{2,1,0:T(8,128)} %bitcast.3, ...), custom_call_target="tpu_custom_call" | custom-call | tf_op jit(solution)/shard_map/tree/pallas_call | solution.py:411
  33.5 4.0 %apply.1 = f32[1024,1024]{1,0:T(8,128)} custom-call(f32[1024,1024]{1,0:T(8,128)S(1)} %get-tuple-element.9.x_ref, bf16[1024,256]{1,0:T(8,128)(2,1)S(1)} %get-tuple-element.10.uh_ref, bf16[1024,256]{1,0:T(8,128)(2,1)S(1)} %get-tuple-element.11.ul_ref, f32[192,1024]{1,0:T(8,128)S(1)} %get-tuple-element.12.q_ref), custom_call_target="tpu_custom_call" | custom-call | tf_op jit(solution)/shard_map/apply/pallas_call | solution.py:441
